TPU v7x, 512 devices: a whole 4x8x8 slice. The times are simulated.
512 devices in a mesh: head: 16 (over x_lo, y), blk: 32 (over z, x_hi, core).
Axes of the slice: x: 4 (x_hi: 2, x_lo: 2; x = x_hi * 2 + x_lo), y: 8, z: 8, core: 2. Of those that a mesh axis runs over, the one named last changes fastest.
Arguments:
- query: bfloat16 [65536, 2048], P(('blk', 'head')), may hold values from -8 to 8
- key_in: bfloat16 [65536, 2048], P(('blk', 'head')), may hold values from -8 to 8
- value: bfloat16 [65536, 2048], P(('blk', 'head')), may hold values from -6 to 6
- grad_out: bfloat16 [65536, 2048], P(('blk', 'head')), may hold values from -96 to 96
Outputs:
- grad_query: bfloat16 [65536, 2048], P(('blk', 'head'))
- grad_key: bfloat16 [65536, 2048], P(('blk', 'head'))
- grad_value: bfloat16 [65536, 2048], P(('blk', 'head'))
All inputs are finite; a program needn't handle non-finite values.
Results may differ from a plain program's by a relative error of at most 0.0052.
Values may be sent and summed in bfloat16 or wider, within the bound.
A program may use at most 64 MiB of HBM per device.

v0:
```python
import jax
import jax.numpy as jnp
from jax import lax
from jax.sharding import PartitionSpec as P

HEADS = 16
HEAD_DIM = 128
HALF = 512
TILE = 512


def with_halo(cells, sides, width):
    for axis, dim in sides:
        count = lax.axis_size(axis)
        ends = count - 1
        head = lax.slice_in_dim(cells, 0, width, axis=dim)
        tail = lax.slice_in_dim(cells, cells.shape[dim] - width, cells.shape[dim], axis=dim)
        cells = jnp.concatenate(
            [
                lax.ppermute(tail, axis, [(i, (i + 1) % count) for i in range(ends)]),
                cells,
                lax.ppermute(head, axis, [((i + 1) % count, i) for i in range(ends)]),
            ],
            axis=dim,
        )
    return cells


def from_behind(array, axis, by):
    devices = lax.axis_size(axis)
    pairs = [(i, i + by) for i in range(devices) if 0 <= i + by < devices]
    return lax.ppermute(array, axis, pairs)


def masked_scores(query_part, key_part, query_first, key_first, seq_total, score_scale):
    raw = (
        jnp.einsum("qhd,khd->hqk", query_part, key_part, preferred_element_type=jnp.float32)
        * score_scale
    )
    query_pos = query_first + jnp.arange(query_part.shape[0], dtype=jnp.int32)
    key_pos = key_first + jnp.arange(key_part.shape[0], dtype=jnp.int32)
    within = jnp.abs(query_pos[:, None] - key_pos[None, :]) <= HALF
    query_ok = (query_pos >= 0) & (query_pos < seq_total)
    key_ok = (key_pos >= 0) & (key_pos < seq_total)
    allowed = within & query_ok[:, None] & key_ok[None, :]
    return jnp.where(allowed[None], raw, -1e30)


def forward_stats(scores, grad_part, value_part):
    row_max = jnp.max(scores, axis=-1)
    shifted = jnp.exp(scores - row_max[..., None])
    denominator = jnp.sum(shifted, axis=-1)
    weighted = jnp.einsum(
        "hqk,khd->hqd", shifted.astype(jnp.bfloat16), value_part, preferred_element_type=jnp.float32
    )
    output_rows = weighted / denominator[..., None]
    log_total = row_max + jnp.log(denominator)
    grad_float = jnp.transpose(grad_part.astype(jnp.float32), (1, 0, 2))
    row_delta = jnp.sum(grad_float * output_rows, axis=-1)
    return (log_total, row_delta)


def grad_parts(scores, log_total, row_delta, grad_part, value_part):
    weights = jnp.exp(scores - log_total[..., None])
    grad_weights = jnp.einsum(
        "qhd,khd->hqk", grad_part, value_part, preferred_element_type=jnp.float32
    )
    grad_scores = weights * (grad_weights - row_delta[..., None])
    return (weights.astype(jnp.bfloat16), grad_scores.astype(jnp.bfloat16))


def shards(query, key_in, value, grad_out):
    heads_dev = HEADS // lax.axis_size("head")
    score_scale = HEAD_DIM ** (-0.5)
    query_t, key_t, value_t, grad_t = (
        lax.all_to_all(query, "head", split_axis=1, concat_axis=0, tiled=True),
        lax.all_to_all(key_in, "head", split_axis=1, concat_axis=0, tiled=True),
        lax.all_to_all(value, "head", split_axis=1, concat_axis=0, tiled=True),
        lax.all_to_all(grad_out, "head", split_axis=1, concat_axis=0, tiled=True),
    )
    row_count = query_t.shape[0]
    feat_width = heads_dev * HEAD_DIM
    seq_total = row_count * lax.axis_size("blk")
    block_base = lax.axis_index("blk") * row_count
    key_span = TILE + 2 * HALF
    tile_count = row_count // TILE
    tile_ids = jnp.arange(tile_count, dtype=jnp.int32)

    def split_heads(matrix):
        return matrix.reshape(matrix.shape[0], heads_dev, HEAD_DIM)

    query_h = split_heads(query_t)
    grad_h = split_heads(grad_t)
    key_pair = jnp.concatenate([key_t, value_t], axis=1)
    pair_ext = with_halo(key_pair, (("blk", 0),), HALF)
    key_ext = split_heads(pair_ext[:, :feat_width])
    value_ext = split_heads(pair_ext[:, feat_width:])

    def tile_step(running, tile_index):
        key_acc, value_acc = running
        offset = tile_index * TILE
        query_part = lax.dynamic_slice_in_dim(query_h, offset, TILE, 0)
        grad_part = lax.dynamic_slice_in_dim(grad_h, offset, TILE, 0)
        key_part = lax.dynamic_slice_in_dim(key_ext, offset, key_span, 0)
        value_part = lax.dynamic_slice_in_dim(value_ext, offset, key_span, 0)
        scores = masked_scores(
            query_part,
            key_part,
            block_base + offset,
            block_base - HALF + offset,
            seq_total,
            score_scale,
        )
        log_total, row_delta = forward_stats(scores, grad_part, value_part)
        weights_low, scores_low = grad_parts(scores, log_total, row_delta, grad_part, value_part)
        add_value = jnp.einsum(
            "hqk,qhd->khd", weights_low, grad_part, preferred_element_type=jnp.float32
        )
        add_key = (
            jnp.einsum("hqk,qhd->khd", scores_low, query_part, preferred_element_type=jnp.float32)
            * score_scale
        )
        add_query = (
            jnp.einsum("hqk,khd->qhd", scores_low, key_part, preferred_element_type=jnp.float32)
            * score_scale
        )
        old_key = lax.dynamic_slice_in_dim(key_acc, offset, key_span, 0)
        old_value = lax.dynamic_slice_in_dim(value_acc, offset, key_span, 0)
        key_acc = lax.dynamic_update_slice_in_dim(key_acc, old_key + add_key, offset, 0)
        value_acc = lax.dynamic_update_slice_in_dim(value_acc, old_value + add_value, offset, 0)
        return ((key_acc, value_acc), (add_query, log_total, row_delta))

    zeros_ext = jnp.zeros((row_count + 2 * HALF, heads_dev, HEAD_DIM), jnp.float32)
    (key_acc, value_acc), (query_tiles, total_tiles, delta_tiles) = lax.scan(
        tile_step, (zeros_ext, zeros_ext), tile_ids
    )
    query_sum = query_tiles.reshape(row_count, heads_dev, HEAD_DIM)
    key_sum = key_acc[HALF : HALF + row_count]
    value_sum = value_acc[HALF : HALF + row_count]
    down_key, down_value = from_behind((key_acc[:HALF], value_acc[:HALF]), "blk", -1)
    up_key, up_value = from_behind(
        (key_acc[HALF + row_count :], value_acc[HALF + row_count :]), "blk", 1
    )
    key_sum = key_sum.at[row_count - HALF :].add(down_key).at[:HALF].add(up_key)
    value_sum = value_sum.at[row_count - HALF :].add(down_value).at[:HALF].add(up_value)

    def merge_heads(stacked):
        return stacked.reshape(row_count, feat_width).astype(jnp.bfloat16)

    grad_query, grad_key, grad_value = (
        lax.all_to_all(merge_heads(query_sum), "head", split_axis=0, concat_axis=1, tiled=True),
        lax.all_to_all(merge_heads(key_sum), "head", split_axis=0, concat_axis=1, tiled=True),
        lax.all_to_all(merge_heads(value_sum), "head", split_axis=0, concat_axis=1, tiled=True),
    )
    return (grad_query, grad_key, grad_value)


def solution(mesh):
    placed = (
        P(("blk", "head"), None),
        P(("blk", "head"), None),
        P(("blk", "head"), None),
        P(("blk", "head"), None),
    )
    return jax.shard_map(
        shards,
        mesh=mesh,
        in_specs=placed,
        out_specs=(P(("blk", "head"), None), P(("blk", "head"), None), P(("blk", "head"), None)),
        check_vma=False,
    )
```

profile of v0, /device:TPU:203, one launch (start us, length us, event | category | flops | bytes accessed | tf_op | source)
XLA Modules:
  0.0 219.3 jit_solution(587740467833863773)
XLA Ops:
  2.6 7.9 %all-to-all-start.1 = ((bf16[128,16,128]{2,0,1:T(8,128)(2,1)}), bf16[128,16,128]{2,0,1:T(8,128)(2,1)S(1)}, u32[]{:S(2)}, u32[]{:S(2)}) async-start(bf16[128,16,128]{2,0,1:T(8,128)(2,1)} %copy_bitcast_fusion.1), calls=%async_computation.1 | async-start | bytes 1048576 | tf_op jit(solution)/shard_map/all_to_all | solution.py:77
  12.5 12.8 %all-to-all-done.1 = bf16[128,16,128]{2,0,1:T(8,128)(2,1)S(1)} async-done(((bf16[128,16,128]{2,0,1:T(8,128)(2,1)}), bf16[128,16,128]{2,0,1:T(8,128)(2,1)S(1)}, u32[]{:S(2)}, u32[]{:S(2)}) %all-to-all-start.1) | async-done | bytes 524320 | tf_op jit(solution)/shard_map/all_to_all | solution.py:77
  25.3 5.1 %all-to-all-start.2 = ((bf16[128,16,128]{2,0,1:T(8,128)(2,1)}), bf16[128,16,128]{2,0,1:T(8,128)(2,1)S(1)}, u32[]{:S(2)}, u32[]{:S(2)}) async-start(bf16[128,16,128]{2,0,1:T(8,128)(2,1)} %copy_bitcast_fusion), calls=%async_computation.2 | async-start | bytes 1048576 | tf_op jit(solution)/shard_map/all_to_all | solution.py:78
  31.4 13.7 %all-to-all-done.2 = bf16[128,16,128]{2,0,1:T(8,128)(2,1)S(1)} async-done(((bf16[128,16,128]{2,0,1:T(8,128)(2,1)}), bf16[128,16,128]{2,0,1:T(8,128)(2,1)S(1)}, u32[]{:S(2)}, u32[]{:S(2)}) %all-to-all-start.2) | async-done | bytes 524320 | tf_op jit(solution)/shard_map/all_to_all | solution.py:78
  45.1 5.1 %all-to-all-start = ((bf16[128,16,128]{0,2,1:T(8,128)(2,1)}), bf16[128,16,128]{0,2,1:T(8,128)(2,1)S(1)}, u32[]{:S(2)}, u32[]{:S(2)}) async-start(bf16[128,16,128]{0,2,1:T(8,128)(2,1)} %bitcast.12), calls=%async_computation | async-start | bytes 1048576 | tf_op jit(solution)/shard_map/all_to_all | solution.py:76
  51.2 13.7 %all-to-all-done = bf16[128,16,128]{0,2,1:T(8,128)(2,1)S(1)} async-done(((bf16[128,16,128]{0,2,1:T(8,128)(2,1)}), bf16[128,16,128]{0,2,1:T(8,128)(2,1)S(1)}, u32[]{:S(2)}, u32[]{:S(2)}) %all-to-all-start) | async-done | bytes 524320 | tf_op jit(solution)/shard_map/all_to_all | solution.py:76
  64.9 4.5 %all-to-all-start.3 = ((bf16[128,16,128]{0,2,1:T(8,128)(2,1)}), bf16[128,16,128]{0,2,1:T(8,128)(2,1)S(1)}, u32[]{:S(2)}, u32[]{:S(2)}) async-start(bf16[128,16,128]{0,2,1:T(8,128)(2,1)} %bitcast.20), calls=%async_computation.3 | async-start | bytes 1048576 | tf_op jit(solution)/shard_map/all_to_all | solution.py:79
  70.1 6.0 %collective-permute-start = (bf16[512,256]{1,0:T(8,128)(2,1)}, bf16[512,256]{1,0:T(8,128)(2,1)S(1)}, u32[]{:S(2)}, u32[]{:S(2)}) collective-permute-start(bf16[512,256]{1,0:T(8,128)(2,1)} %get-tuple-element.227), channel_id=1, source_target_pairs={{0,1},{1,2},{2,3},{3,4},{4,5},{5,6},{6,7},{7,8},{8,9},{9,10},{10,1... | collective-permute-start | bytes 786440 | tf_op jit(solution)/shard_map/ppermute | solution.py:20
  79.0 4.2 %all-to-all-done.3 = bf16[128,16,128]{0,2,1:T(8,128)(2,1)S(1)} async-done(((bf16[128,16,128]{0,2,1:T(8,128)(2,1)}), bf16[128,16,128]{0,2,1:T(8,128)(2,1)S(1)}, u32[]{:S(2)}, u32[]{:S(2)}) %all-to-all-start.3) | async-done | bytes 524320 | tf_op jit(solution)/shard_map/all_to_all | solution.py:79
  84.2 3.4 %collective-permute-done.1 = bf16[512,256]{1,0:T(8,128)(2,1)S(1)} collective-permute-done((bf16[512,256]{1,0:T(8,128)(2,1)S(1)}, bf16[512,256]{1,0:T(8,128)(2,1)S(1)}, u32[]{:S(2)}, u32[]{:S(2)}) %collective-permute-start.1) | collective-permute-done | bytes 262176 | tf_op jit(solution)/shard_map/ppermute | solution.py:22
  90.2 56.1 %while.20 = (s32[]{:T(128)}, f32[3072,1,128]{0,2,1:T(8,128)}, f32[3072,1,128]{0,2,1:T(8,128)S(1)}, bf16[4,512,1,128]{3,1,0,2:T(8,128)(2,1)}, s32[4]{0:T(128)S(1)...) while((s32[]{:T(128)}, f32[3072,1,128]{0,2,1:T(8,128)}, ...), condition=%wide.region_4.5_spmd, body=%wide.region_0.4_spmd.sunk | while | flops 1223107584 | bytes 55358344 | solution.py:134
  96.7 2.8 %fusion.87 = f32[512]{0:T(512)S(1)} fusion(f32[512,1536]{1,0:T(8,128)} %copy-done.1, f32[512]{0:T(512)S(1)} %get-tuple-element.299, bf16[3072,1,128]{2,0,1:T(8,128)(2,1)S(1)} %get-tuple-element.342, s32[]{:T(128)S(6)} %select_n.26, bf16[512,1,128]{0,2,1:T(8,128)(2,1)S(1)} %copy.64, f32[512]{0:T(512)S(1)} %fusion.86), kind=kOutput, calls=%fused_computation.27.clone.1 | convolution fusion | flops 203161088 | bytes 3676164 | tf_op jit(solution)/shard_map/while/body/eval_jaxpr/hqk,khd->hqd/dot_general | solution.py:53
  110.7 2.8 %fusion.87 = f32[512]{0:T(512)S(1)} fusion(f32[512,1536]{1,0:T(8,128)} %copy-done.1, f32[512]{0:T(512)S(1)} %get-tuple-element.299, bf16[3072,1,128]{2,0,1:T(8,128)(2,1)S(1)} %get-tuple-element.342, s32[]{:T(128)S(6)} %select_n.26, bf16[512,1,128]{0,2,1:T(8,128)(2,1)S(1)} %copy.64, f32[512]{0:T(512)S(1)} %fusion.86), kind=kOutput, calls=%fused_computation.27.clone.1 | convolution fusion | flops 203161088 | bytes 3676164 | tf_op jit(solution)/shard_map/while/body/eval_jaxpr/hqk,khd->hqd/dot_general | solution.py:53
  124.8 2.8 %fusion.87 = f32[512]{0:T(512)S(1)} fusion(f32[512,1536]{1,0:T(8,128)} %copy-done.1, f32[512]{0:T(512)S(1)} %get-tuple-element.299, bf16[3072,1,128]{2,0,1:T(8,128)(2,1)S(1)} %get-tuple-element.342, s32[]{:T(128)S(6)} %select_n.26, bf16[512,1,128]{0,2,1:T(8,128)(2,1)S(1)} %copy.64, f32[512]{0:T(512)S(1)} %fusion.86), kind=kOutput, calls=%fused_computation.27.clone.1 | convolution fusion | flops 203161088 | bytes 3676164 | tf_op jit(solution)/shard_map/while/body/eval_jaxpr/hqk,khd->hqd/dot_general | solution.py:53
  138.8 2.8 %fusion.87 = f32[512]{0:T(512)S(1)} fusion(f32[512,1536]{1,0:T(8,128)} %copy-done.1, f32[512]{0:T(512)S(1)} %get-tuple-element.299, bf16[3072,1,128]{2,0,1:T(8,128)(2,1)S(1)} %get-tuple-element.342, s32[]{:T(128)S(6)} %select_n.26, bf16[512,1,128]{0,2,1:T(8,128)(2,1)S(1)} %copy.64, f32[512]{0:T(512)S(1)} %fusion.86), kind=kOutput, calls=%fused_computation.27.clone.1 | convolution fusion | flops 203161088 | bytes 3676164 | tf_op jit(solution)/shard_map/while/body/eval_jaxpr/hqk,khd->hqd/dot_general | solution.py:53
  146.4 6.5 %all-to-all-start.4 = ((bf16[16,128,128]{2,1,0:T(8,128)(2,1)}), bf16[16,128,128]{2,1,0:T(8,128)(2,1)S(1)}, u32[]{:S(2)}, u32[]{:S(2)}) async-start(bf16[16,128,128]{2,1,0:T(8,128)(2,1)} %bitcast.141), calls=%async_computation.4 | async-start | bytes 1048576 | tf_op jit(solution)/shard_map/all_to_all | solution.py:151
  154.8 5.1 %collective-permute-start.5 = (f32[512,1,128]{0,2,1:T(8,128)S(1)}, f32[512,1,128]{0,2,1:T(8,128)S(1)}, u32[]{:S(2)}, u32[]{:S(2)}) collective-permute-start(f32[512,1,128]{0,2,1:T(8,128)S(1)} %get-tuple-element.221), channel_id=1, source_target_pairs={{0,1},{1,2},{2,3},{3,4},{4,5},{5,6},{6,7},{7,8},{8,9},{9,10},{10,1... | collective-permute-start | bytes 786440 | tf_op jit(solution)/shard_map/ppermute | solution.py:32
  160.1 8.7 %collective-permute-done.4 = f32[512,1,128]{0,2,1:T(8,128)S(1)} collective-permute-done((f32[512,1,128]{0,2,1:T(8,128)S(1)}, f32[512,1,128]{0,2,1:T(8,128)S(1)}, u32[]{:S(2)}, u32[]{:S(2)}) %collective-permute-start.4) | collective-permute-done | bytes 262176 | tf_op jit(solution)/shard_map/ppermute | solution.py:32
  170.0 6.3 %all-to-all-start.6 = ((bf16[16,128,128]{2,1,0:T(8,128)(2,1)}), bf16[16,128,128]{2,1,0:T(8,128)(2,1)S(1)}, u32[]{:S(2)}, u32[]{:S(2)}) async-start(bf16[16,128,128]{2,1,0:T(8,128)(2,1)} %bitcast.34), calls=%async_computation.6 | async-start | bytes 1048576 | tf_op jit(solution)/shard_map/all_to_all | solution.py:153
  177.4 3.3 %collective-permute-start.2 = (f32[512,1,128]{0,2,1:T(8,128)S(1)}, f32[512,1,128]{0,2,1:T(8,128)S(1)}, u32[]{:S(2)}, u32[]{:S(2)}) collective-permute-start(f32[512,1,128]{0,2,1:T(8,128)S(1)} %get-tuple-element.224), channel_id=1, source_target_pairs={{1,0},{2,1},{3,2},{4,3},{5,4},{6,5},{7,6},{8,7},{9,8},{10,9},{11,1... | collective-permute-start | bytes 786440 | tf_op jit(solution)/shard_map/ppermute | solution.py:32
  180.7 4.4 %collective-permute-start.3 = (f32[512,1,128]{0,2,1:T(8,128)S(1)}, f32[512,1,128]{0,2,1:T(8,128)S(1)}, u32[]{:S(2)}, u32[]{:S(2)}) collective-permute-start(f32[512,1,128]{0,2,1:T(8,128)S(1)} %get-tuple-element.223), channel_id=1, source_target_pairs={{0,1},{1,2},{2,3},{3,4},{4,5},{5,6},{6,7},{7,8},{8,9},{9,10},{10,1... | collective-permute-start | bytes 786440 | tf_op jit(solution)/shard_map/ppermute | solution.py:32
  186.4 7.7 %collective-permute-done.2 = f32[512,1,128]{0,2,1:T(8,128)S(1)} collective-permute-done((f32[512,1,128]{0,2,1:T(8,128)S(1)}, f32[512,1,128]{0,2,1:T(8,128)S(1)}, u32[]{:S(2)}, u32[]{:S(2)}) %collective-permute-start.2) | collective-permute-done | bytes 262176 | tf_op jit(solution)/shard_map/ppermute | solution.py:32
  196.4 6.9 %all-to-all-start.5 = ((bf16[16,128,128]{2,1,0:T(8,128)(2,1)}), bf16[16,128,128]{2,1,0:T(8,128)(2,1)S(1)}, u32[]{:S(2)}, u32[]{:S(2)}) async-start(bf16[16,128,128]{2,1,0:T(8,128)(2,1)} %bitcast.29), calls=%async_computation.5 | async-start | bytes 1048576 | tf_op jit(solution)/shard_map/all_to_all | solution.py:152
  205.8 12.2 %all-to-all-done.5 = bf16[16,128,128]{2,1,0:T(8,128)(2,1)S(1)} async-done(((bf16[16,128,128]{2,1,0:T(8,128)(2,1)}), bf16[16,128,128]{2,1,0:T(8,128)(2,1)S(1)}, u32[]{:S(2)}, u32[]{:S(2)}) %all-to-all-start.5) | async-done | bytes 524320 | tf_op jit(solution)/shard_map/all_to_all | solution.py:152
  (134 shorter events, 66.9 us)
Async XLA Ops:
  0.6 29.8 %copy-start.4 = (bf16[128,2048]{1,0:T(8,128)(2,1)S(1)}, bf16[128,2048]{1,0:T(8,128)(2,1)}, u32[]{:S(2)}) copy-start(bf16[128,2048]{1,0:T(8,128)(2,1)} %param.14) | copy-start | bytes 1572868
  1.7 48.5 %copy-start.5 = (bf16[128,2048]{1,0:T(8,128)(2,1)S(1)}, bf16[128,2048]{1,0:T(8,128)(2,1)}, u32[]{:S(2)}) copy-start(bf16[128,2048]{1,0:T(8,128)(2,1)} %param.17) | copy-start | bytes 1572868
  2.6 22.7 %all-to-all-start.1 = ((bf16[128,16,128]{2,0,1:T(8,128)(2,1)}), bf16[128,16,128]{2,0,1:T(8,128)(2,1)S(1)}, u32[]{:S(2)}, u32[]{:S(2)}) async-start(bf16[128,16,128]{2,0,1:T(8,128)(2,1)} %copy_bitcast_fusion.1), calls=%async_computation.1 | async-start | bytes 1048576 | tf_op jit(solution)/shard_map/all_to_all | solution.py:77
  25.3 19.8 %all-to-all-start.2 = ((bf16[128,16,128]{2,0,1:T(8,128)(2,1)}), bf16[128,16,128]{2,0,1:T(8,128)(2,1)S(1)}, u32[]{:S(2)}, u32[]{:S(2)}) async-start(bf16[128,16,128]{2,0,1:T(8,128)(2,1)} %copy_bitcast_fusion), calls=%async_computation.2 | async-start | bytes 1048576 | tf_op jit(solution)/shard_map/all_to_all | solution.py:78
  45.1 19.8 %all-to-all-start = ((bf16[128,16,128]{0,2,1:T(8,128)(2,1)}), bf16[128,16,128]{0,2,1:T(8,128)(2,1)S(1)}, u32[]{:S(2)}, u32[]{:S(2)}) async-start(bf16[128,16,128]{0,2,1:T(8,128)(2,1)} %bitcast.12), calls=%async_computation | async-start | bytes 1048576 | tf_op jit(solution)/shard_map/all_to_all | solution.py:76
  64.9 18.3 %all-to-all-start.3 = ((bf16[128,16,128]{0,2,1:T(8,128)(2,1)}), bf16[128,16,128]{0,2,1:T(8,128)(2,1)S(1)}, u32[]{:S(2)}, u32[]{:S(2)}) async-start(bf16[128,16,128]{0,2,1:T(8,128)(2,1)} %bitcast.20), calls=%async_computation.3 | async-start | bytes 1048576 | tf_op jit(solution)/shard_map/all_to_all | solution.py:79
  70.1 14.1 %collective-permute-start = (bf16[512,256]{1,0:T(8,128)(2,1)}, bf16[512,256]{1,0:T(8,128)(2,1)S(1)}, u32[]{:S(2)}, u32[]{:S(2)}) collective-permute-start(bf16[512,256]{1,0:T(8,128)(2,1)} %get-tuple-element.227), channel_id=1, source_target_pairs={{0,1},{1,2},{2,3},{3,4},{4,5},{5,6},{6,7},{7,8},{8,9},{9,10},{10,1... | collective-permute-start | bytes 786440 | tf_op jit(solution)/shard_map/ppermute | solution.py:20
  76.1 11.5 %collective-permute-start.1 = (bf16[512,256]{1,0:T(8,128)(2,1)S(1)}, bf16[512,256]{1,0:T(8,128)(2,1)S(1)}, u32[]{:S(2)}, u32[]{:S(2)}) collective-permute-start(bf16[512,256]{1,0:T(8,128)(2,1)S(1)} %get-tuple-element.228), channel_id=1, source_target_pairs={{1,0},{2,1},{3,2},{4,3},{5,4},{6,5},{7,6},{8,7},{9,8},{10,9},{11,1... | collective-permute-start | bytes 786440 | tf_op jit(solution)/shard_map/ppermute | solution.py:22
  96.7 2.8 %copy-start.2 = (f32[512,1536]{1,0:T(8,128)S(1)}, f32[512,1536]{1,0:T(8,128)}, u32[]{:S(2)}) copy-start(f32[512,1536]{1,0:T(8,128)} %copy-done.1) | copy-start | bytes 9437188 | tf_op jit(solution)/shard_map/while
  99.5 3.3 %copy-start.3 = (bf16[3072,1,128]{2,0,1:T(8,128)(2,1)S(1)}, bf16[3072,1,128]{2,0,1:T(8,128)(2,1)}, u32[]{:S(2)}) copy-start(bf16[3072,1,128]{2,0,1:T(8,128)(2,1)} %get-tuple-element.340) | copy-start | bytes 2359300 | tf_op jit(solution)/shard_map/while
  108.2 1.7 copy-start.1
  110.7 2.8 %copy-start.2 = (f32[512,1536]{1,0:T(8,128)S(1)}, f32[512,1536]{1,0:T(8,128)}, u32[]{:S(2)}) copy-start(f32[512,1536]{1,0:T(8,128)} %copy-done.1) | copy-start | bytes 9437188 | tf_op jit(solution)/shard_map/while
  113.6 3.3 %copy-start.3 = (bf16[3072,1,128]{2,0,1:T(8,128)(2,1)S(1)}, bf16[3072,1,128]{2,0,1:T(8,128)(2,1)}, u32[]{:S(2)}) copy-start(bf16[3072,1,128]{2,0,1:T(8,128)(2,1)} %get-tuple-element.340) | copy-start | bytes 2359300 | tf_op jit(solution)/shard_map/while
  124.8 2.8 %copy-start.2 = (f32[512,1536]{1,0:T(8,128)S(1)}, f32[512,1536]{1,0:T(8,128)}, u32[]{:S(2)}) copy-start(f32[512,1536]{1,0:T(8,128)} %copy-done.1) | copy-start | bytes 9437188 | tf_op jit(solution)/shard_map/while
  127.6 3.3 %copy-start.3 = (bf16[3072,1,128]{2,0,1:T(8,128)(2,1)S(1)}, bf16[3072,1,128]{2,0,1:T(8,128)(2,1)}, u32[]{:S(2)}) copy-start(bf16[3072,1,128]{2,0,1:T(8,128)(2,1)} %get-tuple-element.340) | copy-start | bytes 2359300 | tf_op jit(solution)/shard_map/while
  138.8 2.8 %copy-start.2 = (f32[512,1536]{1,0:T(8,128)S(1)}, f32[512,1536]{1,0:T(8,128)}, u32[]{:S(2)}) copy-start(f32[512,1536]{1,0:T(8,128)} %copy-done.1) | copy-start | bytes 9437188 | tf_op jit(solution)/shard_map/while
  141.6 3.3 %copy-start.3 = (bf16[3072,1,128]{2,0,1:T(8,128)(2,1)S(1)}, bf16[3072,1,128]{2,0,1:T(8,128)(2,1)}, u32[]{:S(2)}) copy-start(bf16[3072,1,128]{2,0,1:T(8,128)(2,1)} %get-tuple-element.340) | copy-start | bytes 2359300 | tf_op jit(solution)/shard_map/while
  146.4 23.6 %all-to-all-start.4 = ((bf16[16,128,128]{2,1,0:T(8,128)(2,1)}), bf16[16,128,128]{2,1,0:T(8,128)(2,1)S(1)}, u32[]{:S(2)}, u32[]{:S(2)}) async-start(bf16[16,128,128]{2,1,0:T(8,128)(2,1)} %bitcast.141), calls=%async_computation.4 | async-start | bytes 1048576 | tf_op jit(solution)/shard_map/all_to_all | solution.py:151
  152.9 15.8 %collective-permute-start.4 = (f32[512,1,128]{0,2,1:T(8,128)S(1)}, f32[512,1,128]{0,2,1:T(8,128)S(1)}, u32[]{:S(2)}, u32[]{:S(2)}) collective-permute-start(f32[512,1,128]{0,2,1:T(8,128)S(1)} %get-tuple-element.222), channel_id=1, source_target_pairs={{1,0},{2,1},{3,2},{4,3},{5,4},{6,5},{7,6},{8,7},{9,8},{10,9},{11,1... | collective-permute-start | bytes 786440 | tf_op jit(solution)/shard_map/ppermute | solution.py:32
  154.8 14.1 %collective-permute-start.5 = (f32[512,1,128]{0,2,1:T(8,128)S(1)}, f32[512,1,128]{0,2,1:T(8,128)S(1)}, u32[]{:S(2)}, u32[]{:S(2)}) collective-permute-start(f32[512,1,128]{0,2,1:T(8,128)S(1)} %get-tuple-element.221), channel_id=1, source_target_pairs={{0,1},{1,2},{2,3},{3,4},{4,5},{5,6},{6,7},{7,8},{8,9},{9,10},{10,1... | collective-permute-start | bytes 786440 | tf_op jit(solution)/shard_map/ppermute | solution.py:32
  170.0 26.3 %all-to-all-start.6 = ((bf16[16,128,128]{2,1,0:T(8,128)(2,1)}), bf16[16,128,128]{2,1,0:T(8,128)(2,1)S(1)}, u32[]{:S(2)}, u32[]{:S(2)}) async-start(bf16[16,128,128]{2,1,0:T(8,128)(2,1)} %bitcast.34), calls=%async_computation.6 | async-start | bytes 1048576 | tf_op jit(solution)/shard_map/all_to_all | solution.py:153
  177.4 16.7 %collective-permute-start.2 = (f32[512,1,128]{0,2,1:T(8,128)S(1)}, f32[512,1,128]{0,2,1:T(8,128)S(1)}, u32[]{:S(2)}, u32[]{:S(2)}) collective-permute-start(f32[512,1,128]{0,2,1:T(8,128)S(1)} %get-tuple-element.224), channel_id=1, source_target_pairs={{1,0},{2,1},{3,2},{4,3},{5,4},{6,5},{7,6},{8,7},{9,8},{10,9},{11,1... | collective-permute-start | bytes 786440 | tf_op jit(solution)/shard_map/ppermute | solution.py:32
  180.7 14.5 %collective-permute-start.3 = (f32[512,1,128]{0,2,1:T(8,128)S(1)}, f32[512,1,128]{0,2,1:T(8,128)S(1)}, u32[]{:S(2)}, u32[]{:S(2)}) collective-permute-start(f32[512,1,128]{0,2,1:T(8,128)S(1)} %get-tuple-element.223), channel_id=1, source_target_pairs={{0,1},{1,2},{2,3},{3,4},{4,5},{5,6},{6,7},{7,8},{8,9},{9,10},{10,1... | collective-permute-start | bytes 786440 | tf_op jit(solution)/shard_map/ppermute | solution.py:32
  196.4 21.6 %all-to-all-start.5 = ((bf16[16,128,128]{2,1,0:T(8,128)(2,1)}), bf16[16,128,128]{2,1,0:T(8,128)(2,1)S(1)}, u32[]{:S(2)}, u32[]{:S(2)}) async-start(bf16[16,128,128]{2,1,0:T(8,128)(2,1)} %bitcast.29), calls=%async_computation.5 | async-start | bytes 1048576 | tf_op jit(solution)/shard_map/all_to_all | solution.py:152
  (4 other events, 6.1 us)
where the time goes:
time: 221 us; the launch traced here: 219 us
  waiting for transfers between devices  76.3 us (35%)
  starting transfers between devices  64.9 us (29%)
  matrix products  40 us (18%)
  local copies, waits for them, and re-layouts  29.7 us (13%)
  other arithmetic  4.53 us (2%)
  loops' own time  2.99 us (1%)
    ppermute x4, waiting for transfers between devices, from_behind(): return lax.ppermute(array, axis, pairs)  16.4 us
    ppermute x4, starting transfers between devices, from_behind(): return lax.ppermute(array, axis, pairs)  14.8 us
    all_to_all x1, waiting for transfers between devices, shards(): lax.all_to_all(value, 'head', split_axis=1, concat_axis=0, tiled=True)  13.7 us
    all_to_all x1, waiting for transfers between devices, shards(): lax.all_to_all(query, 'head', split_axis=1, concat_axis=0, tiled=True)  13.7 us
    all_to_all x1, waiting for transfers between devices, shards(): lax.all_to_all(key_in, 'head', split_axis=1, concat_axis=0, tiled=True)  12.8 us
    all_to_all x1, waiting for transfers between devices, shards(): lax.all_to_all(merge_heads(key_sum), 'head', split_axis=0, concat_axis=1,...  12.2 us
    dot_general x4, matrix products, forward_stats(): jnp.einsum('hqk,khd->hqd', shifted.astype(jnp.bfloat16), value_part, pref...  11.1 us
    dot_general x4, matrix products, tile_step(): jnp.einsum('hqk,qhd->khd', scores_low, query_part, preferred_element_type...  10.2 us
  transfers between devices with their start and end apart: 13, of which 8 were waited for; matrix products, arithmetic and copies ran while one was open for 7% of the time, Pallas kernels for 0%

commit v1 on v0

v1 whole, which is shorter than its diff:
```python
import functools

import jax
import jax.numpy as jnp
from jax import lax
from jax.experimental import pallas as pl
from jax.experimental.pallas import tpu as pltpu
from jax.sharding import PartitionSpec as P

HEADS = 16
DIM = 128
HALF = 512
T = 256
CHUNKS = (T + 2 * HALF) // T
LOG2E = 1.4426950408889634
MESH = pl.DeviceIdType.MESH


def dot_nt(a, b):
    return lax.dot_general(a, b, (((1,), (1,)), ((), ())), preferred_element_type=jnp.float32)


def dot_nn(a, b):
    return jnp.dot(a, b, preferred_element_type=jnp.float32)


def kernel(
    heads, blks, part,
    q_in, k_in, v_in, g_in, dq_out, dk_out, dv_out,
    q_t, g_t, k_e, v_e, k_tr, s_buf, d_buf, dk_acc, dv_acc, dq_t, dk_t, dv_t, half_out, half_in,
    send, recv, hsend, hrecv, gsend, grecv, local,
):
    rows = heads * part
    tiles = rows // T
    scale = DIM ** (-0.5)
    me = lax.axis_index("head")
    blk = lax.axis_index("blk")
    left = lax.rem(blk + blks - 1, blks)
    right = lax.rem(blk + 1, blks)

    barrier = pltpu.get_barrier_semaphore()

    def greet(d, carry):
        pl.semaphore_signal(barrier, inc=1, device_id={"head": lax.rem(me + d, heads)}, device_id_type=MESH)
        return carry

    lax.fori_loop(1, heads, greet, 0)
    pl.semaphore_signal(barrier, inc=1, device_id={"blk": left}, device_id_type=MESH)
    pl.semaphore_signal(barrier, inc=1, device_id={"blk": right}, device_id_type=MESH)
    pl.semaphore_wait(barrier, heads + 1)

    def lanes(index):
        return pl.ds(pl.multiple_of(index * DIM, DIM), DIM)

    def span(index, base=0):
        return pl.ds(pl.multiple_of(base + index * part, part), part)

    ins = ((k_in, k_e, HALF), (v_in, v_e, HALF), (q_in, q_t, 0), (g_in, g_t, 0))

    def in_copy(n, peer, source):
        src, dst, base = ins[n]
        return pltpu.make_async_remote_copy(
            src_ref=src.at[:, lanes(peer)],
            dst_ref=dst.at[span(source, base)],
            send_sem=send.at[n, peer],
            recv_sem=recv.at[n, source],
            device_id={"head": peer},
            device_id_type=MESH,
        )

    own = []
    for n, (src, dst, base) in enumerate(ins):
        copy = pltpu.make_async_copy(src.at[:, lanes(me)], dst.at[span(me, base)], local.at[n])
        copy.start()
        own.append(copy)

    for n in range(4):
        def start_in(d, carry, n=n):
            in_copy(n, lax.rem(me + d, heads), me).start()
            return carry

        lax.fori_loop(1, heads, start_in, 0)

    def wait_in(n):
        def body(d, carry):
            source = lax.rem(me + d, heads)
            in_copy(n, source, source).wait_recv()
            return carry

        own[n].wait()
        lax.fori_loop(1, heads, body, 0)

    def halo(slot, ext, src_row, dst_row, target):
        return pltpu.make_async_remote_copy(
            src_ref=ext.at[pl.ds(src_row, HALF)],
            dst_ref=ext.at[pl.ds(dst_row, HALF)],
            send_sem=hsend.at[slot],
            recv_sem=hrecv.at[slot],
            device_id={"blk": target},
            device_id_type=MESH,
        )

    halos = []
    for n, ext in ((0, k_e), (1, v_e)):
        wait_in(n)
        halos.append(halo(2 * n, ext, rows, 0, right))
        halos.append(halo(2 * n + 1, ext, HALF, HALF + rows, left))
        halos[-2].start()
        halos[-1].start()

    dk_acc[...] = jnp.zeros_like(dk_acc)
    dv_acc[...] = jnp.zeros_like(dv_acc)
    for copy in halos:
        copy.wait_recv()

    def turn(c, carry):
        k_tr[c] = k_e[pl.ds(pl.multiple_of(c * T, T), T), :].astype(jnp.float32).T.astype(jnp.bfloat16)
        return carry

    lax.fori_loop(0, tiles + CHUNKS - 1, turn, 0)
    wait_in(2)
    wait_in(3)

    def out_copy(n, src, dst, peer, source):
        return pltpu.make_async_remote_copy(
            src_ref=src.at[span(peer)],
            dst_ref=dst.at[:, lanes(source)],
            send_sem=send.at[n, peer],
            recv_sem=recv.at[n, source],
            device_id={"head": peer},
            device_id_type=MESH,
        )

    outs = ((4, dq_t, dq_out), (5, dk_t, dk_out), (6, dv_t, dv_out))

    def give(index, peer):
        n, src, dst = outs[index]

        @pl.when(peer != me)
        def _():
            out_copy(n, src, dst, peer, me).start()

        @pl.when(peer == me)
        def _():
            pltpu.make_async_copy(src.at[span(me)], dst.at[:, lanes(me)], local.at[n]).start()

    def send_query(i):
        t = lax.rem(i + me, tiles)
        for half in range(T // part):
            give(0, t * (T // part) + half)

    row = lax.broadcasted_iota(jnp.int32, (T, T), 0)
    col = lax.broadcasted_iota(jnp.int32, (T, T), 1)
    seq_total = rows * blks
    fold = scale * LOG2E

    def tile_step(i, carry):
        t = lax.rem(i + me, tiles)
        offset = pl.multiple_of(t * T, T)
        q = q_t[pl.ds(offset, T), :]
        g = g_t[pl.ds(offset, T), :]
        top = jnp.full((1, T), -1e30, jnp.float32)
        biases = []
        for c in range(CHUNKS):
            keys = pl.ds(pl.multiple_of(offset + c * T, T), T)
            s = dot_nt(k_e[keys, :], q)
            if c == 0:
                s = jnp.where(row >= col, s, -1e30)
            if c == CHUNKS - 1:
                s = jnp.where(row <= col, s, -1e30)
            first = blk * rows + offset + (c * T - HALF)
            bias = jnp.where((first >= 0) & (first < seq_total), 0.0, 1e30).astype(jnp.float32)
            biases.append(bias)
            top = jnp.maximum(top, jnp.max(s, axis=0, keepdims=True) - bias)
            s_buf[c] = s
        total = jnp.zeros((1, T), jnp.float32)
        delta = jnp.zeros((1, T), jnp.float32)
        for c in range(CHUNKS):
            keys = pl.ds(pl.multiple_of(offset + c * T, T), T)
            p = jnp.exp2((s_buf[c] - (top + biases[c])) * fold)
            dp = dot_nt(v_e[keys, :], g)
            total = total + jnp.sum(p, axis=0, keepdims=True)
            delta = delta + jnp.sum(p * dp, axis=0, keepdims=True)
            s_buf[c] = p
            d_buf[c] = dp
        inv = 1.0 / total
        delta = delta * inv
        dq = jnp.zeros((DIM, T), jnp.float32)
        for c in range(CHUNKS):
            keys = pl.ds(pl.multiple_of(offset + c * T, T), T)
            w = s_buf[c] * inv
            ds = (w * (d_buf[c] - delta)).astype(jnp.bfloat16)
            dv_acc[keys, :] += dot_nn(w.astype(jnp.bfloat16), g)
            dk_acc[keys, :] += dot_nn(ds, q)
            dq = dq + dot_nn(k_tr[t + c], ds)
        dq_t[pl.ds(offset, T), :] = (dq * scale).T.astype(jnp.bfloat16)

        @pl.when(i > 0)
        def _():
            send_query(i - 1)

        return carry

    lax.fori_loop(0, tiles, tile_step, 0)

    for slot, acc, at, factor in (
        (0, dk_acc, 0, scale), (1, dv_acc, 0, 1.0),
        (2, dk_acc, HALF + rows, scale), (3, dv_acc, HALF + rows, 1.0),
    ):
        half_out[slot] = (acc[pl.ds(at, HALF), :] * factor).astype(jnp.bfloat16)
    send_query(tiles - 1)
    mid = rows - 2 * HALF
    dk_t[pl.ds(HALF, mid), :] = (dk_acc[pl.ds(2 * HALF, mid), :] * scale).astype(jnp.bfloat16)
    dv_t[pl.ds(HALF, mid), :] = dv_acc[pl.ds(2 * HALF, mid), :].astype(jnp.bfloat16)
    backs = []
    for slot in range(4):
        copy = pltpu.make_async_remote_copy(
            src_ref=half_out.at[slot],
            dst_ref=half_in.at[slot],
            send_sem=gsend.at[slot],
            recv_sem=grecv.at[slot],
            device_id={"blk": left if slot < 2 else right},
            device_id_type=MESH,
        )
        copy.start()
        backs.append(copy)

    edge = HALF // part
    inner = heads - 2 * edge

    def send_inner(d, carry):
        peer = edge + lax.rem(me + d, inner)
        give(1, peer)
        give(2, peer)
        return carry

    lax.fori_loop(0, inner, send_inner, 0)
    for copy in backs:
        copy.wait_recv()
    for slot, at, out, acc, factor in (
        (0, rows - HALF, dk_t, dk_acc, scale), (1, rows - HALF, dv_t, dv_acc, 1.0),
        (2, 0, dk_t, dk_acc, scale), (3, 0, dv_t, dv_acc, 1.0),
    ):
        mine = acc[pl.ds(at + HALF, HALF), :] * factor
        out[pl.ds(at, HALF), :] = (mine + half_in[slot].astype(jnp.float32)).astype(jnp.bfloat16)

    def send_outer(d, carry):
        peer = lax.rem(heads - edge + lax.rem(me + d, 2 * edge), heads)
        give(1, peer)
        give(2, peer)
        return carry

    lax.fori_loop(0, 2 * edge, send_outer, 0)

    for n, src, dst in outs:
        pltpu.make_async_copy(src.at[span(me)], dst.at[:, lanes(me)], local.at[n]).wait()

    def finish(d, carry):
        other = lax.rem(me + d, heads)
        for n in range(4):
            in_copy(n, other, me).wait_send()
        for n, src, dst in outs:
            out_copy(n, src, dst, other, me).wait_send()
            out_copy(n, src, dst, other, other).wait_recv()
        return carry

    lax.fori_loop(1, heads, finish, 0)
    for copy in halos + backs:
        copy.wait_send()


def shards(query, key_in, value, grad_out):
    heads = lax.axis_size("head")
    blks = lax.axis_size("blk")
    part = query.shape[0]
    rows = heads * part
    wide = rows + 2 * HALF
    bf16, f32 = jnp.bfloat16, jnp.float32
    shape = jax.ShapeDtypeStruct(query.shape, bf16)
    any_spec = pl.BlockSpec(memory_space=pl.ANY)
    dma = pltpu.SemaphoreType.DMA
    return pl.pallas_call(
        functools.partial(kernel, heads, blks, part),
        out_shape=(shape, shape, shape),
        in_specs=[any_spec] * 4,
        out_specs=(any_spec,) * 3,
        scratch_shapes=[
            pltpu.VMEM((rows, DIM), bf16),
            pltpu.VMEM((rows, DIM), bf16),
            pltpu.VMEM((wide, DIM), bf16),
            pltpu.VMEM((wide, DIM), bf16),
            pltpu.VMEM((wide // T, DIM, T), bf16),
            pltpu.VMEM((CHUNKS, T, T), f32),
            pltpu.VMEM((CHUNKS, T, T), f32),
            pltpu.VMEM((wide, DIM), f32),
            pltpu.VMEM((wide, DIM), f32),
            pltpu.VMEM((rows, DIM), bf16),
            pltpu.VMEM((rows, DIM), bf16),
            pltpu.VMEM((rows, DIM), bf16),
            pltpu.VMEM((4, HALF, DIM), bf16),
            pltpu.VMEM((4, HALF, DIM), bf16),
            dma((7, heads)),
            dma((7, heads)),
            dma((4,)),
            dma((4,)),
            dma((4,)),
            dma((4,)),
            dma((7,)),
        ],
        compiler_params=pltpu.CompilerParams(collective_id=0, has_side_effects=True),
    )(query, key_in, value, grad_out)


def solution(mesh):
    placed = P(("blk", "head"), None)
    return jax.shard_map(
        shards,
        mesh=mesh,
        in_specs=(placed,) * 4,
        out_specs=(placed,) * 3,
        check_vma=False,
    )
```

time: 221 us -> 105 us (0.48)
  the two profiles are of different devices: /device:TPU:203 before, /device:TPU:201 now
where the time goes in v1:
time: 105 us
  Pallas kernels  100 us (95%)
  local copies, waits for them, and re-layouts  3.97 us (4%)
    pallas_call x1, Pallas kernels, shards(): pl.pallas_call(functools.partial(kernel, heads, blks, part), out_shape=(s...  100 us
    unnamed x7, local copies, waits for them, and re-layouts  3.97 us

profile of v1, /device:TPU:201, one launch (start us, length us, event | category | flops | bytes accessed | tf_op | source)
XLA Modules:
  0.0 105.0 jit_solution(5748855183903749769)
XLA Ops:
  0.6 100.4 %shard_map.67 = (bf16[128,2048]{1,0:T(8,128)(2,1)}, bf16[128,2048]{1,0:T(8,128)(2,1)}, bf16[128,2048]{1,0:T(8,128)(2,1)}) custom-call(bf16[128,2048]{1,0:T(8,128)(2,1)} %q_in.1, bf16[128,2048]{1,0:T(8,128)(2,1)} %k_in.1, bf16[128,2048]{1,0:T(8,128)(2,1)} %v_in.1, bf16[128,2048]{1,0:T(8,128)(2,1)} %g_in.1), custom_call_target="tpu_custom_call" | custom-call | tf_op jit(solution)/shard_map/pallas_call | solution.py:282
  101.0 0.0 copy-start.1
  101.0 1.9 %copy.10 = bf16[128,2048]{1,0:T(8,128)(2,1)} copy(bf16[128,2048]{1,0:T(8,128)(2,1)} %get-tuple-element.6) | data formatting | bytes 1048576
  103.0 0.0 copy-done.1
  103.0 0.0 copy-start
  103.0 0.8 copy.11
  103.8 0.4 copy-done
  104.2 0.8 copy.12
Async XLA Ops:
  101.0 2.0 %copy-start.1 = (bf16[128,2048]{1,0:T(8,128)(2,1)S(1)}, bf16[128,2048]{1,0:T(8,128)(2,1)}, u32[]{:S(2)}) copy-start(bf16[128,2048]{1,0:T(8,128)(2,1)} %get-tuple-element.7) | copy-start | bytes 1572868
  103.0 1.2 %copy-start = (bf16[128,2048]{1,0:T(8,128)(2,1)S(1)}, bf16[128,2048]{1,0:T(8,128)(2,1)}, u32[]{:S(2)}) copy-start(bf16[128,2048]{1,0:T(8,128)(2,1)} %get-tuple-element.8) | copy-start | bytes 1572868

commit v2 on v1

--- a/solution.py
+++ b/solution.py
@@ -27,7 +27,7 @@
 def kernel(
     heads, blks, part,
     q_in, k_in, v_in, g_in, dq_out, dk_out, dv_out,
-    q_t, g_t, k_e, v_e, k_tr, s_buf, d_buf, dk_acc, dv_acc, dq_t, dk_t, dv_t, half_out, half_in,
+    q_t, g_t, k_e, v_e, k_tr, s_buf, d_buf, inv_buf, dk_acc, dv_acc, dq_t, dk_t, dv_t, half_out, half_in,
     send, recv, hsend, hrecv, gsend, grecv, local,
 ):
     rows = heads * part
@@ -55,7 +55,7 @@
     def span(index, base=0):
         return pl.ds(pl.multiple_of(base + index * part, part), part)
 
-    ins = ((k_in, k_e, HALF), (v_in, v_e, HALF), (q_in, q_t, 0), (g_in, g_t, 0))
+    ins = ((k_in, k_e, HALF), (q_in, q_t, 0), (v_in, v_e, HALF), (g_in, g_t, 0))
 
     def in_copy(n, peer, source):
         src, dst, base = ins[n]
@@ -100,17 +100,17 @@
             device_id_type=MESH,
         )
 
-    halos = []
-    for n, ext in ((0, k_e), (1, v_e)):
+    def spread(n, slot, ext):
         wait_in(n)
-        halos.append(halo(2 * n, ext, rows, 0, right))
-        halos.append(halo(2 * n + 1, ext, HALF, HALF + rows, left))
-        halos[-2].start()
-        halos[-1].start()
-
+        pair = [halo(slot, ext, rows, 0, right), halo(slot + 1, ext, HALF, HALF + rows, left)]
+        for copy in pair:
+            copy.start()
+        return pair
+
+    key_halos = spread(0, 0, k_e)
     dk_acc[...] = jnp.zeros_like(dk_acc)
     dv_acc[...] = jnp.zeros_like(dv_acc)
-    for copy in halos:
+    for copy in key_halos:
         copy.wait_recv()
 
     def turn(c, carry):
@@ -118,8 +118,7 @@
         return carry
 
     lax.fori_loop(0, tiles + CHUNKS - 1, turn, 0)
-    wait_in(2)
-    wait_in(3)
+    wait_in(1)
 
     def out_copy(n, src, dst, peer, source):
         return pltpu.make_async_remote_copy(
@@ -154,13 +153,11 @@
     seq_total = rows * blks
     fold = scale * LOG2E
 
-    def tile_step(i, carry):
-        t = lax.rem(i + me, tiles)
+    def score_step(t, carry):
         offset = pl.multiple_of(t * T, T)
         q = q_t[pl.ds(offset, T), :]
-        g = g_t[pl.ds(offset, T), :]
         top = jnp.full((1, T), -1e30, jnp.float32)
-        biases = []
+        biases, parts = [], []
         for c in range(CHUNKS):
             keys = pl.ds(pl.multiple_of(offset + c * T, T), T)
             s = dot_nt(k_e[keys, :], q)
@@ -172,23 +169,40 @@
             bias = jnp.where((first >= 0) & (first < seq_total), 0.0, 1e30).astype(jnp.float32)
             biases.append(bias)
             top = jnp.maximum(top, jnp.max(s, axis=0, keepdims=True) - bias)
-            s_buf[c] = s
+            parts.append(s)
         total = jnp.zeros((1, T), jnp.float32)
+        for c in range(CHUNKS):
+            p = jnp.exp2((parts[c] - (top + biases[c])) * fold)
+            total = total + jnp.sum(p, axis=0, keepdims=True)
+            s_buf[t, c] = p
+        inv_buf[t] = 1.0 / total
+        return carry
+
+    lax.fori_loop(0, tiles, score_step, 0)
+
+    value_halos = spread(2, 2, v_e)
+    for copy in value_halos:
+        copy.wait_recv()
+    wait_in(3)
+    halos = key_halos + value_halos
+
+    def tile_step(i, carry):
+        t = lax.rem(i + me, tiles)
+        offset = pl.multiple_of(t * T, T)
+        q = q_t[pl.ds(offset, T), :]
+        g = g_t[pl.ds(offset, T), :]
+        inv = inv_buf[t]
         delta = jnp.zeros((1, T), jnp.float32)
         for c in range(CHUNKS):
             keys = pl.ds(pl.multiple_of(offset + c * T, T), T)
-            p = jnp.exp2((s_buf[c] - (top + biases[c])) * fold)
             dp = dot_nt(v_e[keys, :], g)
-            total = total + jnp.sum(p, axis=0, keepdims=True)
-            delta = delta + jnp.sum(p * dp, axis=0, keepdims=True)
-            s_buf[c] = p
+            delta = delta + jnp.sum(s_buf[t, c] * dp, axis=0, keepdims=True)
             d_buf[c] = dp
-        inv = 1.0 / total
         delta = delta * inv
         dq = jnp.zeros((DIM, T), jnp.float32)
         for c in range(CHUNKS):
             keys = pl.ds(pl.multiple_of(offset + c * T, T), T)
-            w = s_buf[c] * inv
+            w = s_buf[t, c] * inv
             ds = (w * (d_buf[c] - delta)).astype(jnp.bfloat16)
             dv_acc[keys, :] += dot_nn(w.astype(jnp.bfloat16), g)
             dk_acc[keys, :] += dot_nn(ds, q)
@@ -269,6 +283,20 @@
         copy.wait_send()
 
 
+def settle(*refs):
+    froms, tos, holds = refs[:3], refs[3:6], refs[6:9]
+    into, onto = refs[9:]
+    reads = [pltpu.make_async_copy(a, b, into.at[i]) for i, (a, b) in enumerate(zip(froms, holds))]
+    writes = [pltpu.make_async_copy(b, c, onto.at[i]) for i, (b, c) in enumerate(zip(holds, tos))]
+    for read in reads:
+        read.start()
+    for read, write in zip(reads, writes):
+        read.wait()
+        write.start()
+    for write in writes:
+        write.wait()
+
+
 def shards(query, key_in, value, grad_out):
     heads = lax.axis_size("head")
     blks = lax.axis_size("blk")
@@ -279,7 +307,7 @@
     shape = jax.ShapeDtypeStruct(query.shape, bf16)
     any_spec = pl.BlockSpec(memory_space=pl.ANY)
     dma = pltpu.SemaphoreType.DMA
-    return pl.pallas_call(
+    grads = pl.pallas_call(
         functools.partial(kernel, heads, blks, part),
         out_shape=(shape, shape, shape),
         in_specs=[any_spec] * 4,
@@ -290,8 +318,9 @@
             pltpu.VMEM((wide, DIM), bf16),
             pltpu.VMEM((wide, DIM), bf16),
             pltpu.VMEM((wide // T, DIM, T), bf16),
+            pltpu.VMEM((rows // T, CHUNKS, T, T), f32),
             pltpu.VMEM((CHUNKS, T, T), f32),
-            pltpu.VMEM((CHUNKS, T, T), f32),
+            pltpu.VMEM((rows // T, 1, T), f32),
             pltpu.VMEM((wide, DIM), f32),
             pltpu.VMEM((wide, DIM), f32),
             pltpu.VMEM((rows, DIM), bf16),
@@ -309,6 +338,13 @@
         ],
         compiler_params=pltpu.CompilerParams(collective_id=0, has_side_effects=True),
     )(query, key_in, value, grad_out)
+    return pl.pallas_call(
+        settle,
+        out_shape=(shape, shape, shape),
+        in_specs=[any_spec] * 3,
+        out_specs=(any_spec,) * 3,
+        scratch_shapes=[pltpu.VMEM(query.shape, bf16)] * 3 + [dma((3,)), dma((3,))],
+    )(*grads)
 
 
 def solution(mesh):

time: 105 us -> 102 us (0.971)
  the two profiles are of different devices: /device:TPU:201 before, /device:TPU:205 now
where the time goes in v2:
time: 102 us
  Pallas kernels  101 us (99%)
    pallas_call x1, Pallas kernels, shards(): pl.pallas_call(functools.partial(kernel, heads, blks, part), out_shape=(s...  98.8 us
    pallas_call x1, Pallas kernels, shards(): pl.pallas_call(settle, out_shape=(shape, shape, shape), in_specs=[any_spe...  2.23 us

profile of v2, /device:TPU:205, one launch (start us, length us, event | category | flops | bytes accessed | tf_op | source)
XLA Modules:
  0.0 101.7 jit_solution(17578534925974928008)
XLA Ops:
  0.6 98.8 %shard_map.67 = (bf16[128,2048]{1,0:T(8,128)(2,1)}, bf16[128,2048]{1,0:T(8,128)(2,1)}, bf16[128,2048]{1,0:T(8,128)(2,1)}) custom-call(bf16[128,2048]{1,0:T(8,128)(2,1)} %q_in.1, bf16[128,2048]{1,0:T(8,128)(2,1)} %k_in.1, bf16[128,2048]{1,0:T(8,128)(2,1)} %v_in.1, bf16[128,2048]{1,0:T(8,128)(2,1)} %g_in.1), custom_call_target="tpu_custom_call" | custom-call | tf_op jit(solution)/shard_map/pallas_call | solution.py:310
  99.4 2.2 %shard_map.68 = (bf16[128,2048]{1,0:T(8,128)(2,1)}, bf16[128,2048]{1,0:T(8,128)(2,1)}, bf16[128,2048]{1,0:T(8,128)(2,1)}) custom-call(bf16[128,2048]{1,0:T(8,128)(2,1)} %get-tuple-element.6.refs_0_, bf16[128,2048]{1,0:T(8,128)(2,1)} %get-tuple-element.7.refs_1_, bf16[128,2048]{1,0:T(8,128)(2,1)} %get-tuple-element.8.refs_2_), custom_call_target="tpu_custom_call" | custom-call | tf_op jit(solution)/shard_map/pallas_call | solution.py:341

commit v3 on v2

--- a/solution.py
+++ b/solution.py
@@ -143,8 +143,11 @@
         def _():
             pltpu.make_async_copy(src.at[span(me)], dst.at[:, lanes(me)], local.at[n]).start()
 
+    def pick(i):
+        return lax.rem((me + heads - 1) // 2 + tiles - i, tiles)
+
     def send_query(i):
-        t = lax.rem(i + me, tiles)
+        t = pick(i)
         for half in range(T // part):
             give(0, t * (T // part) + half)
 
@@ -183,11 +186,18 @@
     value_halos = spread(2, 2, v_e)
     for copy in value_halos:
         copy.wait_recv()
-    wait_in(3)
+    own[3].wait()
     halos = key_halos + value_halos
 
     def tile_step(i, carry):
-        t = lax.rem(i + me, tiles)
+        t = pick(i)
+        for half in range(T // part):
+            source = t * (T // part) + half
+
+            @pl.when(source != me)
+            def _():
+                in_copy(3, source, source).wait_recv()
+
         offset = pl.multiple_of(t * T, T)
         q = q_t[pl.ds(offset, T), :]
         g = g_t[pl.ds(offset, T), :]

time: 102 us -> 101 us (level)
  the two profiles are of different devices: /device:TPU:205 before, /device:TPU:1 now
where the time goes in v3:
time: 101 us
  Pallas kernels  99.9 us (99%)
    pallas_call x1, Pallas kernels, shards(): pl.pallas_call(functools.partial(kernel, heads, blks, part), out_shape=(s...  97.7 us
    pallas_call x1, Pallas kernels, shards(): pl.pallas_call(settle, out_shape=(shape, shape, shape), in_specs=[any_spe...  2.23 us

profile of v3, /device:TPU:1, one launch (start us, length us, event | category | flops | bytes accessed | tf_op | source)
XLA Modules:
  0.0 100.6 jit_solution(8181997706571585343)
XLA Ops:
  0.6 97.7 %shard_map.67 = (bf16[128,2048]{1,0:T(8,128)(2,1)}, bf16[128,2048]{1,0:T(8,128)(2,1)}, bf16[128,2048]{1,0:T(8,128)(2,1)}) custom-call(bf16[128,2048]{1,0:T(8,128)(2,1)} %q_in.1, bf16[128,2048]{1,0:T(8,128)(2,1)} %k_in.1, bf16[128,2048]{1,0:T(8,128)(2,1)} %v_in.1, bf16[128,2048]{1,0:T(8,128)(2,1)} %g_in.1), custom_call_target="tpu_custom_call" | custom-call | tf_op jit(solution)/shard_map/pallas_call | solution.py:320
  98.3 2.2 %shard_map.68 = (bf16[128,2048]{1,0:T(8,128)(2,1)}, bf16[128,2048]{1,0:T(8,128)(2,1)}, bf16[128,2048]{1,0:T(8,128)(2,1)}) custom-call(bf16[128,2048]{1,0:T(8,128)(2,1)} %get-tuple-element.6.refs_0_, bf16[128,2048]{1,0:T(8,128)(2,1)} %get-tuple-element.7.refs_1_, bf16[128,2048]{1,0:T(8,128)(2,1)} %get-tuple-element.8.refs_2_), custom_call_target="tpu_custom_call" | custom-call | tf_op jit(solution)/shard_map/pallas_call | solution.py:351
